TPU v7x, 128 devices: a whole 4x4x4 slice. The times are simulated.
128 devices in a mesh: gx: 8 (over y, core), gy: 16 (over z, x).
Axes of the slice: x: 4, y: 4, z: 4, core: 2. Of those that a mesh axis runs over, the one named last changes fastest.
Arguments:
- thermal_anomaly: float32 [32, 256, 2048], P(None, 'gx', 'gy'), may hold values from -6 to 6
- ambient_diffusion: bfloat16 [256, 2048], P('gx', 'gy'), may hold values from 0.019897461 to 0.25
- solar_light: bfloat16 [256, 2048], P('gx', 'gy'), may hold values from 0.5 to 4
- sea_tile_flags: int32 [8, 16, 64], P('gx', 'gy'), may hold values 0 or 1
- flooded_layer_tally: int32 [8, 16, 64], P('gx', 'gy'), may hold values from 1 to 32
- tile_holder_rank: int32 [8, 16, 64, 1], P('gx', 'gy'), may hold values from 0 to 15; in each aligned block of 64 rows (0 to 63, 64 to 127, ..., all dimensions but the last counted through in order) at most 8 rows name the same one
- solute_amounts: float32 [8, 16, 128, 8, 2048], P('gx', 'gy'), may hold values from 0.09 to 11
- reaction_rates: float32 [8, 8], replicated, may hold values from -0.2 to 0.5
Outputs:
- thermal_final: float32 [32, 256, 2048], P(None, 'gx', 'gy')
- solute_final: float32 [8, 16, 128, 8, 2048], P('gx', 'gy')
Inputs may be any that keep to these rules, and one draw needn't show every extreme that they name: `tile_holder_rank`: among the 64 blocks of one device, at most 8 name the same owner, a bound that some block reaches of them.
All inputs are finite; a program needn't handle non-finite values. No bound on the sum of `sea_tile_flags` on one device may be relied on, other than what follows from the above.
Results may differ from a plain program's by a relative error of at most 0.0003.
Values may be sent and summed in bfloat16 or wider, within the bound.
A program may use at most 128 MiB of HBM per device.

v0:
```python
import jax
import jax.numpy as jnp
from jax import lax
from jax.sharding import Mesh
from jax.sharding import PartitionSpec as P

GX_GY = ("gx_0", "gx_1", "gy_0", "gy_1")
GX = ("gx_0", "gx_1")
GY = ("gy_0", "gy_1")
NU_COEF = 0.2
STEP_DT = 0.05
ATTEN_WATER = 0.06
ATTEN_CHL = 0.05
WARMING_SCALE = 0.5
GROWTH_TEMP = 0.063


def with_halo(shard, sides, width):
    edges = {}
    for axis, dim in sides:
        count, length = (lax.axis_size(axis), shard.shape[dim])
        up = [(i, (i + 1) % count) for i in range(count - 1)]
        last = lax.slice_in_dim(shard, length - width, length, axis=dim)
        initial = lax.slice_in_dim(shard, 0, width, axis=dim)
        edges[dim] = (
            lax.ppermute(last, axis, up),
            lax.ppermute(initial, axis, [(b, a) for a, b in up]),
        )
    done = []
    for _, dim in sides:
        low, high = edges[dim]
        around = [(width, width) if d in done else (0, 0) for d in range(shard.ndim)]
        shard = jnp.concatenate([jnp.pad(low, around), shard, jnp.pad(high, around)], axis=dim)
        done.append(dim)
    return shard


def by_axis(shard, axes):
    for axis in axes:
        shard = lax.psum(shard, axis)
    return shard


def masked_step(field, within_layer):
    center = field[:, 1:-1, 1:-1]
    span_east = center.shape[1]
    span_north = center.shape[2]
    total = jnp.zeros_like(center)
    for first, second in ((0, 1), (2, 1), (1, 0), (1, 2)):
        near = field[:, first : first + span_east, second : second + span_north]
        total = total + within_layer[:, first : first + span_east, second : second + span_north] * (
            near - center
        )
    return center + NU_COEF * within_layer[:, 1:-1, 1:-1] * total


def level_below(values):
    return jnp.concatenate([values[..., 64:], values[..., -64:]], axis=-1)


def level_above_zero(values):
    return jnp.concatenate([jnp.zeros_like(values[..., :64]), values[..., :-64]], axis=-1)


def level_prefix(values, layer_tally):
    running = values
    reach = 1
    while reach < layer_tally:
        moved = jnp.concatenate(
            [jnp.zeros_like(running[..., : 64 * reach]), running[..., : -64 * reach]], axis=-1
        )
        running = running + moved
        reach = reach * 2
    return running


def spread_levels(column_values, layer_tally):
    return jnp.tile(column_values, (1, layer_tally))


def flat_mixer(temp_flat, kbg_flat):
    return (kbg_flat * (1.0 + 0.5 * jnp.tanh(temp_flat - level_below(temp_flat)))).astype(
        jnp.bfloat16
    )


def flat_validity(tile_amount, flat_width):
    levels = lax.broadcasted_iota(jnp.int32, (1, flat_width), 1) // 64
    valid = (levels < tile_amount[:, None]).astype(jnp.float32)
    active = (levels + 1 < tile_amount[:, None]).astype(jnp.float32)
    return (valid, active)


def totals(amounts_on_chip, valid):
    return jnp.sum(amounts_on_chip * valid[:, None], axis=(0, 2))


def column_step(
    temp_flat, kappa_flat, surface, valid, active, amounts_on_chip, reaction_rates, layer_tally
):
    atten = ATTEN_WATER + ATTEN_CHL * amounts_on_chip[:, 0]
    cumul = level_prefix(atten, layer_tally)
    top = surface * jnp.exp(-(cumul - atten))
    bottom = surface * jnp.exp(-cumul)
    heat = (valid * (top - bottom)).astype(jnp.bfloat16)
    growth = jnp.exp(GROWTH_TEMP * temp_flat.astype(jnp.float32)) * top / (top + 1.0)
    mixed = jnp.einsum(
        "rs,nsf->nrf", reaction_rates, amounts_on_chip, precision=lax.Precision.HIGHEST
    )
    flux = (kappa_flat.astype(jnp.float32) * active)[:, None] * (
        level_below(amounts_on_chip) - amounts_on_chip
    )
    new = amounts_on_chip + valid[:, None] * STEP_DT * (
        flux - level_above_zero(flux) + growth[:, None] * mixed
    )
    return (new, heat)


def plane_blocks(field, blocks_x, blocks_y):
    return (
        field.reshape(blocks_x, 8, blocks_y, 8)
        .transpose(0, 2, 1, 3)
        .reshape(blocks_x * blocks_y, 64)
    )


def on_device(
    thermal_anomaly,
    ambient_diffusion,
    solar_light,
    sea_tile_flags,
    flooded_layer_tally,
    tile_holder_rank,
    solute_amounts,
    reaction_rates,
):
    layer_tally = thermal_anomaly.shape[0]
    span_east = thermal_anomaly.shape[1]
    span_north = thermal_anomaly.shape[2]
    blocks_x = span_east // 8
    blocks_y = span_north // 8
    tile_summation = blocks_x * blocks_y
    flat_width = layer_tally * 64
    depth_block = (sea_tile_flags * flooded_layer_tally).reshape(tile_summation)
    cell_count = jnp.repeat(
        jnp.repeat(depth_block.reshape(blocks_x, blocks_y), 8, axis=0), 8, axis=1
    )
    level_idx = lax.broadcasted_iota(jnp.int32, (layer_tally, 1, 1), 0)
    joined = jnp.concatenate([thermal_anomaly, cell_count[None].astype(jnp.float32)], axis=0)
    padded = with_halo(joined, ((GX, 1), (GY, 2)), 1)
    inside_pad = (level_idx.astype(jnp.float32) < padded[layer_tally : layer_tally + 1]).astype(
        jnp.float32
    )
    advanced_verticals = masked_step(padded[:layer_tally], inside_pad)
    dispatched = advanced_verticals.astype(jnp.bfloat16)
    thermal_tiles = (
        dispatched.reshape(layer_tally, blocks_x, 8, blocks_y, 8)
        .transpose(1, 3, 0, 2, 4)
        .reshape(tile_summation, flat_width)
    )
    ambient_diffusion_tiles = plane_blocks(ambient_diffusion, blocks_x, blocks_y)
    shortwave_blocks = plane_blocks(solar_light, blocks_x, blocks_y)
    diffusion_each_tile = flat_mixer(
        thermal_tiles.astype(jnp.float32),
        spread_levels(ambient_diffusion_tiles.astype(jnp.float32), layer_tally),
    )
    payload = jnp.concatenate([thermal_tiles, diffusion_each_tile, shortwave_blocks], axis=1)
    holder_chip = tile_holder_rank.reshape(tile_summation)
    order = jnp.arange(tile_summation, dtype=jnp.int32)
    same = (holder_chip[:, None] == holder_chip[None, :]) & (order[None, :] < order[:, None])
    rank = jnp.sum(same.astype(jnp.int32), axis=1)
    position_summation = solute_amounts.shape[2]
    device_groups = lax.axis_size(GY)
    slot_limit = position_summation // device_groups
    target_owner = holder_chip * slot_limit + rank
    selection_mask = (
        lax.broadcasted_iota(jnp.int32, (position_summation, tile_summation), 0)
        == target_owner[None, :]
    )
    select_b = selection_mask.astype(jnp.bfloat16)
    packed = jnp.einsum("sb,bf->sf", select_b, payload, preferred_element_type=jnp.float32).astype(
        jnp.bfloat16
    )
    packed_count = jnp.sum(selection_mask.astype(jnp.int32) * depth_block[None, :], axis=1)
    arrived_tiles, received_count = (
        lax.all_to_all(
            packed.reshape(device_groups, slot_limit, packed.shape[1]),
            GY,
            split_axis=0,
            concat_axis=0,
            tiled=True,
        ),
        lax.all_to_all(
            packed_count.reshape(device_groups, slot_limit),
            GY,
            split_axis=0,
            concat_axis=0,
            tiled=True,
        ),
    )
    arrived_tiles = arrived_tiles.reshape(position_summation, arrived_tiles.shape[2])
    tile_amount = received_count.reshape(position_summation)
    thermal_at_position = arrived_tiles[:, :flat_width]
    diffusion_at_position = arrived_tiles[:, flat_width : 2 * flat_width]
    solar_at_position = arrived_tiles[:, 2 * flat_width :]
    surface = spread_levels(solar_at_position.astype(jnp.float32), layer_tally)
    amounts_on_chip = solute_amounts.reshape(
        position_summation, solute_amounts.shape[3], flat_width
    )
    valid, active = flat_validity(tile_amount, flat_width)
    old_local = totals(amounts_on_chip, valid)
    cells_local = jnp.sum(valid)
    new, heat = column_step(
        thermal_at_position,
        diffusion_at_position,
        surface,
        valid,
        active,
        amounts_on_chip,
        reaction_rates,
        layer_tally,
    )
    old_total, cells, new_total = (
        by_axis(old_local, GX_GY),
        by_axis(cells_local, GX_GY),
        by_axis(totals(new, valid), GX_GY),
    )
    shift = (old_total - new_total) / jnp.maximum(cells, 1.0)
    solute_final = jnp.where(
        valid[:, None] > 0, new + shift[None, :, None], amounts_on_chip
    ).reshape(solute_amounts.shape)
    returned_blocks = lax.all_to_all(
        heat.reshape(device_groups, slot_limit, flat_width),
        GY,
        split_axis=0,
        concat_axis=0,
        tiled=True,
    )
    returned_blocks = returned_blocks.reshape(position_summation, flat_width)
    heat_blocks = jnp.einsum(
        "sb,sf->bf", select_b, returned_blocks, preferred_element_type=jnp.float32
    )
    warming_each_site = (
        heat_blocks.reshape(blocks_x, blocks_y, layer_tally, 8, 8)
        .transpose(2, 0, 3, 1, 4)
        .reshape(layer_tally, span_east, span_north)
    )
    thermal_final = advanced_verticals + WARMING_SCALE * warming_each_site
    return (thermal_final, solute_final)


def solution(mesh):
    finer = Mesh(mesh.devices.reshape(4, 2, 4, 4), ("gx_0", "gx_1", "gy_0", "gy_1"))
    in_specs = (
        P(None, GX, GY),
        P(GX, GY),
        P(GX, GY),
        P(GX, GY, None),
        P(GX, GY, None),
        P(GX, GY, None, None),
        P(GX, GY, None, None, None),
        P(),
    )
    out_specs = (P(None, GX, GY), P(GX, GY, None, None, None))
    return jax.shard_map(
        on_device, mesh=finer, in_specs=in_specs, out_specs=out_specs, check_vma=False
    )
```

profile of v0, /device:TPU:0, one launch (start us, length us, event | category | flops | bytes accessed | tf_op | source)
XLA Modules:
  0.0 178.2 jit_solution(17803232174242923997)
XLA Ops:
  1.6 1.5 fusion.17
  3.5 3.5 %collective-permute-start = (f32[33,32,1]{0,1,2:T(8,128)S(1)}, f32[33,32,1]{0,1,2:T(8,128)S(1)}, u32[]{:S(2)}, u32[]{:S(2)}) collective-permute-start(f32[33,32,1]{0,1,2:T(8,128)S(1)} %copy.106), channel_id=1, source_target_pairs={{0,1},{1,2},{2,3},{3,4},{4,5},{5,6},{6,7},{7,8},{8,9},{9,10},{10,1... | collective-permute-start | bytes 12680 | tf_op jit(solution)/shard_map/ppermute | solution.py:26
  9.7 1.5 collective-permute-start.1
  15.5 8.9 %all-to-all-start = ((s32[16,1,8]{2,1,0:T(1,128)}), s32[16,1,8]{2,1,0:T(1,128)S(1)}, u32[]{:S(2)}, u32[]{:S(2)}) async-start(s32[16,1,8]{2,1,0:T(1,128)} %bitcast.8), calls=%async_computation | async-start | bytes 16384 | tf_op jit(solution)/shard_map/all_to_all | solution.py:193
  24.4 4.8 %fusion.9 = f32[128,1,2048]{2,1,0:T(1,128)S(1)} fusion(f32[128,8,2048]{2,1,0:T(8,128)} %bitcast.77), kind=kLoop, calls=%fused_computation.21 | loop fusion | flops 524288 | bytes 2097152 | tf_op jit(solution)/shard_map/add | solution.py:101
  36.6 2.0 %fusion.45 = (bf16[32,32,128]{2,1,0:T(8,128)(2,1)}, f32[32,32,128]{2,1,0:T(8,128)}) fusion(f32[32,32,128]{2,1,0:T(8,128)S(1)} %copy-done.1, f32[33,34,1]{2,1,0:T(8,128)S(1)} %pad.14, f32[33,1,128]{2,1,0:T(1,128)S(1)} %collective-permute-done.2, f32[1,32,128]{2,1,0:T(8,128)S(1)} %copy.105, f32[33,1,128]{2,1,0:T(1,128)S(1)} %collective-permute-done.1, ...), kind=kLoop, calls=%fused_computation.108 | loop fusion | flops 3538944 | bytes 3991312 | tf_op jit(solution)/shard_map/convert_element_type | solution.py:155
  38.6 2.3 %copy.111 = bf16[32,32,128]{0,2,1:T(8,128)(2,1)} copy(bf16[32,32,128]{2,1,0:T(8,128)(2,1)} %get-tuple-element.20) | data formatting | bytes 524288 | tf_op jit(solution)/shard_map/convert_element_type | solution.py:155
  40.9 4.9 %copy.112 = bf16[4,16,32,8,8]{1,0,4,3,2:T(4,128)(2,1)S(1)} copy(bf16[4,16,32,8,8]{2,4,1,3,0:T(8,128)(2,1)} %bitcast.83) | data formatting | bytes 524288 | tf_op jit(solution)/shard_map/transpose | solution.py:158
  45.9 1.7 reshape.250
  50.9 2.5 %convolution_convert_fusion = bf16[128,4160]{0,1:T(8,128)(2,1)} fusion(bf16[64,64]{0,1:T(8,128)(2,1)S(1)} %reshape.252, bf16[64,2048]{0,1:T(8,128)(2,1)S(1)} %fusion.14, bf16[64,2048]{0,1:T(8,128)(2,1)} %reshape.250, s32[64]{0:T(128)S(1)} %multiply_add_fusion), kind=kOutput, calls=%fused_computation.8 | convolution fusion | flops 70295552 | bytes 1597696 | tf_op jit(solution)/shard_map/sb,bf->sf/dot_general | solution.py:181
  53.5 2.4 %copy.115 = bf16[128,4160]{1,0:T(8,128)(2,1)} copy(bf16[128,4160]{0,1:T(8,128)(2,1)} %convolution_convert_fusion) | data formatting | bytes 2129920 | tf_op jit(solution)/shard_map/convert_element_type | solution.py:181
  55.8 7.3 %all-to-all-start.1 = ((bf16[16,8,4160]{2,1,0:T(8,128)(2,1)}), bf16[16,8,4160]{2,1,0:T(8,128)(2,1)}, u32[]{:S(2)}, u32[]{:S(2)}) async-start(bf16[16,8,4160]{2,1,0:T(8,128)(2,1)} %bitcast.82), calls=%async_computation.1 | async-start | bytes 2162688 | tf_op jit(solution)/shard_map/all_to_all | solution.py:186
  63.3 9.4 %slice.148 = f32[128,8,1984]{2,1,0:T(8,128)} slice(f32[128,8,2048]{2,1,0:T(8,128)} %bitcast.78), slice={[0:128], [0:8], [64:2048]} | slice | bytes 16252928 | tf_op jit(solution)/shard_map/slice | solution.py:58
  72.6 2.1 %slice.149 = f32[128,8,64]{2,1,0:T(8,128)} slice(f32[128,8,2048]{2,1,0:T(8,128)} %bitcast.79), slice={[0:128], [0:8], [1984:2048]} | slice | bytes 524288 | tf_op jit(solution)/shard_map/slice | solution.py:58
  78.1 2.9 %all-to-all-done.1 = bf16[16,8,4160]{2,1,0:T(8,128)(2,1)} async-done(((bf16[16,8,4160]{2,1,0:T(8,128)(2,1)}), bf16[16,8,4160]{2,1,0:T(8,128)(2,1)}, u32[]{:S(2)}, u32[]{:S(2)}) %all-to-all-start.1) | async-done | bytes 1064992 | tf_op jit(solution)/shard_map/all_to_all | solution.py:186
  83.3 4.9 %add_divide_fusion = (f32[128,2048]{1,0:T(8,128)S(1)}, bf16[16,8,2048]{2,1,0:T(8,128)(2,1)}, f32[128,2048]{1,0:T(8,128)}, f32[]{:T(128)}, f32[128,2048]{1,0:T(8,128)S(1)}) fusion(f32[128,2048]{1,0:T(8,128)} %copy.117, f32[128,2048]{1,0:T(8,128)} %copy-done.4, f32[128,1024]{1,0:T(8,128)} %slice.146, bf16[128,4160]{1,0:T(8,128)(2,1)} %bitcast.15, ...), kind=kLoop, calls=%fused_computation.29 | loop fusion | flops 5505023 | bytes 8405508 | tf_op jit(solution)/shard_map/div | solution.py:106
  88.3 4.6 %all-to-all-start.2 = ((bf16[16,8,2048]{2,1,0:T(8,128)(2,1)}), bf16[16,8,2048]{2,1,0:T(8,128)(2,1)S(1)}, u32[]{:S(2)}, u32[]{:S(2)}) async-start(bf16[16,8,2048]{2,1,0:T(8,128)(2,1)} %get-tuple-element.23), calls=%async_computation.2 | async-start | bytes 1048576 | tf_op jit(solution)/shard_map/all_to_all | solution.py:232
  92.9 8.0 %fusion = f32[128,8,2048]{2,1,0:T(8,128)S(1)} fusion(f32[128,8,64]{2,1,0:T(8,128)} %slice.149, f32[128,8,1984]{2,1,0:T(8,128)} %slice.148, f32[128,2048]{1,0:T(8,128)} %get-tuple-element.24, f32[1,1,128,8,2048]{4,3,2,1,0:T(8,128)} %param.14), kind=kLoop, calls=%fused_computation.1 | loop fusion | flops 6291456 | bytes 26214400 | tf_op jit(solution)/shard_map/mul | solution.py:110
  100.9 24.2 %multiply_reduce_fusion = (f32[8]{0:T(128)S(1)}, f32[8]{0:T(128)S(1)}, f32[128,8,2048]{2,1,0:T(8,128)}) fusion(f32[128,2048]{1,0:T(8,128)S(1)} %copy-done.5, f32[1,1,128,8,2048]{4,3,2,1,0:T(8,128)} %param.14, f32[8,8]{1,0:T(8,128)S(1)} %copy-done, f32[128,2048]{1,0:T(8,128)S(1)} %get-tuple-element.22, f32[128,8,2048]{2,1,0:T(8,128)S(1)} %fusion, ...), kind=kOutput, calls=%fused_computation.6 | convolution fusion | flops 220200944 | bytes 36438336 | tf_op jit(solution)/shard_map/rs,nsf->nrf/dot_general | solution.py:107
  125.1 13.9 %all-reduce.10 = (f32[8]{0:T(128)S(1)}, f32[8]{0:T(128)S(1)}, f32[]{:T(128)}) all-reduce(f32[8]{0:T(128)S(1)} %get-tuple-element.7, f32[8]{0:T(128)S(1)} %get-tuple-element.6, f32[]{:T(128)} %get-tuple-element.29), channel_id=1, replica_groups=mesh['gx_0'=4,'gx_1'=2,'gy_0'=4,'gy_1'=4] {'gx_0'}, use_global_device_ids=true, to_apply=%region_3.4 | all-reduce | flops 17 | bytes 136 | tf_op jit(solution)/shard_map/psum | solution.py:40
  139.0 3.1 %all-reduce.11 = (f32[8]{0:T(128)S(1)}, f32[8]{0:T(128)S(1)}, f32[]{:T(128)}) all-reduce(f32[8]{0:T(128)S(1)} %get-tuple-element.14, f32[8]{0:T(128)S(1)} %get-tuple-element.15, f32[]{:T(128)} %get-tuple-element.16), channel_id=1, replica_groups=mesh['gx_0'=4,'gx_1'=2,'gy_0'=4,'gy_1'=4] {'gx_1'}, use_global_device_ids=true, to_apply=%region_4.5 | all-reduce | flops 17 | bytes 136 | tf_op jit(solution)/shard_map/psum | solution.py:40
  142.1 11.5 %all-reduce.9 = (f32[8]{0:T(128)S(1)}, f32[8]{0:T(128)S(1)}, f32[]{:T(128)}) all-reduce(f32[8]{0:T(128)S(1)} %get-tuple-element.17, f32[8]{0:T(128)S(1)} %get-tuple-element.18, f32[]{:T(128)} %get-tuple-element.19), channel_id=1, replica_groups=mesh['gx_0'=4,'gx_1'=2,'gy_0'=4,'gy_1'=4] {'gy_0'}, use_global_device_ids=true, to_apply=%region_5.6 | all-reduce | flops 17 | bytes 136 | tf_op jit(solution)/shard_map/psum | solution.py:40
  153.6 11.0 %all-reduce.8 = (f32[8]{0:T(128)S(1)}, f32[8]{0:T(128)S(1)}, f32[]{:T(128)}) all-reduce(f32[8]{0:T(128)S(1)} %get-tuple-element.11, f32[8]{0:T(128)S(1)} %get-tuple-element.12, f32[]{:T(128)} %get-tuple-element.13), channel_id=1, replica_groups=mesh['gx_0'=4,'gx_1'=2,'gy_0'=4,'gy_1'=4] {'gy_1'}, use_global_device_ids=true, to_apply=%region_6.7 | all-reduce | flops 17 | bytes 136 | tf_op jit(solution)/shard_map/psum | solution.py:40
  165.2 9.3 %select_bitcast_fusion = f32[1,1,128,8,2048]{4,3,2,1,0:T(8,128)} fusion(f32[128,8,2048]{2,1,0:T(8,128)} %get-tuple-element.33, f32[8]{0:T(128)S(1)} %subtract_divide_fusion, pred[128,2048]{1,0:T(8,128)(4,1)S(1)} %get-tuple-element.31, f32[1,1,128,8,2048]{4,3,2,1,0:T(8,128)} %param.14), kind=kLoop, calls=%fused_computation.5 | loop fusion | flops 4194304 | bytes 25428000 | tf_op jit(solution)/shard_map/reshape | solution.py:231
  (82 shorter events, 28.5 us)
Async XLA Ops:
  0.6 100.2 %copy-start = (f32[8,8]{1,0:T(8,128)S(1)}, f32[8,8]{1,0:T(8,128)}, u32[]{:S(2)}) copy-start(f32[8,8]{1,0:T(8,128)} %param.15) | copy-start | bytes 772
  3.5 27.9 %collective-permute-start = (f32[33,32,1]{0,1,2:T(8,128)S(1)}, f32[33,32,1]{0,1,2:T(8,128)S(1)}, u32[]{:S(2)}, u32[]{:S(2)}) collective-permute-start(f32[33,32,1]{0,1,2:T(8,128)S(1)} %copy.106), channel_id=1, source_target_pairs={{0,1},{1,2},{2,3},{3,4},{4,5},{5,6},{6,7},{7,8},{8,9},{9,10},{10,1... | collective-permute-start | bytes 12680 | tf_op jit(solution)/shard_map/ppermute | solution.py:26
  7.4 26.4 %collective-permute-start.3 = (f32[33,32,1]{0,1,2:T(8,128)S(1)}, f32[33,32,1]{0,1,2:T(8,128)S(1)}, u32[]{:S(2)}, u32[]{:S(2)}) collective-permute-start(f32[33,32,1]{0,1,2:T(8,128)S(1)} %copy.108), channel_id=1, source_target_pairs={{1,0},{2,1},{3,2},{4,3},{5,4},{6,5},{7,6},{8,7},{9,8},{10,9},{11,1... | collective-permute-start | bytes 12680 | tf_op jit(solution)/shard_map/ppermute | solution.py:27
  9.7 26.6 %collective-permute-start.1 = (f32[33,1,128]{2,1,0:T(1,128)S(1)}, f32[33,1,128]{2,1,0:T(1,128)S(1)}, u32[]{:S(2)}, u32[]{:S(2)}) collective-permute-start(f32[33,1,128]{2,1,0:T(1,128)S(1)} %get-tuple-element.27), channel_id=1, source_target_pairs={{0,16},{16,32},{32,48},{48,64},{64,80},{80,96},{96,112},{1,17},{17... | collective-permute-start | bytes 50696 | tf_op jit(solution)/shard_map/ppermute | solution.py:26
  11.2 25.2 %collective-permute-start.2 = (f32[33,1,128]{2,1,0:T(1,128)S(1)}, f32[33,1,128]{2,1,0:T(1,128)S(1)}, u32[]{:S(2)}, u32[]{:S(2)}) collective-permute-start(f32[33,1,128]{2,1,0:T(1,128)S(1)} %get-tuple-element.28), channel_id=1, source_target_pairs={{16,0},{32,16},{48,32},{64,48},{80,64},{96,80},{112,96},{17,1},{33... | collective-permute-start | bytes 50696 | tf_op jit(solution)/shard_map/ppermute | solution.py:27
  15.5 40.3 %all-to-all-start = ((s32[16,1,8]{2,1,0:T(1,128)}), s32[16,1,8]{2,1,0:T(1,128)S(1)}, u32[]{:S(2)}, u32[]{:S(2)}) async-start(s32[16,1,8]{2,1,0:T(1,128)} %bitcast.8), calls=%async_computation | async-start | bytes 16384 | tf_op jit(solution)/shard_map/all_to_all | solution.py:193
  24.4 6.1 %copy-start.7 = (bf16[32,128]{1,0:T(8,128)(2,1)S(1)}, bf16[32,128]{1,0:T(8,128)(2,1)}, u32[]{:S(2)}) copy-start(bf16[32,128]{1,0:T(8,128)(2,1)} %param.9) | copy-start | bytes 24580
  29.2 1.7 copy-start.8
  30.1 6.3 %copy-start.1 = (f32[32,32,128]{2,1,0:T(8,128)S(1)}, f32[32,32,128]{2,1,0:T(8,128)}, u32[]{:S(2)}) copy-start(f32[32,32,128]{2,1,0:T(8,128)} %param.8) | copy-start | bytes 1572868
  30.5 10.5 %copy-start.2 = (f32[128,2048]{1,0:T(8,128)}, f32[128,2048]{1,0:T(8,128)S(1)}, u32[]{:S(2)}) copy-start(f32[128,2048]{1,0:T(8,128)S(1)} %pad_add_fusion.2) | copy-start | bytes 3145732
  47.7 15.5 %copy-start.3 = (f32[128,2048]{1,0:T(8,128)S(1)}, f32[128,2048]{1,0:T(8,128)}, u32[]{:S(2)}) copy-start(f32[128,2048]{1,0:T(8,128)} %copy-done.2) | copy-start | bytes 3145732
  47.7 15.5 %slice-start = ((f32[128,2048]{1,0:T(8,128)}), f32[128,1536]{1,0:T(8,128)S(1)}, s32[]{:S(2)}) async-start(f32[128,2048]{1,0:T(8,128)} %copy-done.2), calls=%async_computation.3 | async-start | bytes 1572864 | tf_op jit(solution)/shard_map/slice | solution.py:70
  55.8 25.1 %all-to-all-start.1 = ((bf16[16,8,4160]{2,1,0:T(8,128)(2,1)}), bf16[16,8,4160]{2,1,0:T(8,128)(2,1)}, u32[]{:S(2)}, u32[]{:S(2)}) async-start(bf16[16,8,4160]{2,1,0:T(8,128)(2,1)} %bitcast.82), calls=%async_computation.1 | async-start | bytes 2162688 | tf_op jit(solution)/shard_map/all_to_all | solution.py:186
  63.2 11.5 %copy-start.4 = (f32[128,2048]{1,0:T(8,128)}, f32[128,2048]{1,0:T(8,128)S(1)}, u32[]{:S(2)}) copy-start(f32[128,2048]{1,0:T(8,128)S(1)} %pad_add_fusion.1) | copy-start | bytes 3145732
  88.3 86.2 %all-to-all-start.2 = ((bf16[16,8,2048]{2,1,0:T(8,128)(2,1)}), bf16[16,8,2048]{2,1,0:T(8,128)(2,1)S(1)}, u32[]{:S(2)}, u32[]{:S(2)}) async-start(bf16[16,8,2048]{2,1,0:T(8,128)(2,1)} %get-tuple-element.23), calls=%async_computation.2 | async-start | bytes 1048576 | tf_op jit(solution)/shard_map/all_to_all | solution.py:232
  92.9 8.0 %copy-start.5 = (f32[128,2048]{1,0:T(8,128)S(1)}, f32[128,2048]{1,0:T(8,128)}, u32[]{:S(2)}) copy-start(f32[128,2048]{1,0:T(8,128)} %get-tuple-element.32) | copy-start | bytes 3145732
  174.4 2.9 %copy-start.6 = (f32[32,32,128]{2,1,0:T(8,128)S(1)}, f32[32,32,128]{2,1,0:T(8,128)}, u32[]{:S(2)}) copy-start(f32[32,32,128]{2,1,0:T(8,128)} %get-tuple-element.21) | copy-start | bytes 1572868
where the time goes:
time: 179 us; the launch traced here: 178 us
  other arithmetic  39.7 us (22%)
  blocking collectives  39.5 us (22%)
  local copies, waits for them, and re-layouts  38.5 us (22%)
  starting transfers between devices  28.2 us (16%)
  matrix products  27.8 us (16%)
  waiting for transfers between devices  2.92 us (2%)
    psum x4, blocking collectives, by_axis(): shard = lax.psum(shard, axis)  39.5 us
    dot_general x1, matrix products, column_step(): jnp.einsum('rs,nsf->nrf', reaction_rates, amounts_on_chip, precision=lax....  24.2 us
    slice x4, local copies, waits for them, and re-layouts, level_below(): return jnp.concatenate([values[..., 64:], values[..., -64:]], axis=-1)  13.4 us
    reshape x1, other arithmetic, on_device(): solute_final = jnp.where(valid[:, None] > 0, new + shift[None, :, None],...  9.28 us
    all_to_all x1, starting transfers between devices, on_device(): lax.all_to_all(packed_count.reshape(device_groups, slot_limit), GY, split...  8.86 us
    mul x1, other arithmetic, column_step(): (kappa_flat.astype(jnp.float32) * active)[:, None]  7.96 us
    all_to_all x1, starting transfers between devices, on_device(): lax.all_to_all(packed.reshape(device_groups, slot_limit, packed.shape[1])...  7.27 us
    transpose x1, local copies, waits for them, and re-layouts, on_device(): thermal_tiles = dispatched.reshape(layer_tally, blocks_x, 8, blocks_y, 8)...  4.95 us
  transfers between devices with their start and end apart: 7, of which 1 were waited for; matrix products, arithmetic and copies ran while one was open for 51% of the time, Pallas kernels for 0%

commit v1 on v0

--- a/solution.py
+++ b/solution.py
@@ -37,7 +37,7 @@
 
 def by_axis(shard, axes):
     for axis in axes:
-        shard = lax.psum(shard, axis)
+        shard = lax.all_gather(shard, axis).sum(axis=0)
     return shard
 
 

time: 179 us -> 185 us (1.034)
  local copies, waits for them, and re-layouts: 38.5 us -> 49 us
  waiting for transfers between devices: 2.92 us -> 0.02 us
  between operations: 1.63 us -> 4.44 us
  matrix products: 27.8 us -> 25.2 us
  blocking collectives: 39.5 us -> 37.5 us
    psum x4 -> x0, blocking collectives: 39.5 us -> none  [by_axis(): shard = lax.psum(shard, axis)]
    unnamed x0 -> x4, blocking collectives: none -> 37.5 us
    unnamed x20 -> x60, local copies, waits for them, and re-layouts: 0.47 us -> 10.4 us
    all_to_all x1, waiting for transfers between devices: 2.91 us -> 0.01 us  [on_device(): lax.all_to_all(packed.reshape(device_groups, slot_limit, packed.shape[1])...]
    reduce_sum x0 -> x12, other arithmetic: none -> 2.78 us  [by_axis(): shard = lax.all_gather(shard, axis).sum(axis=0)]
    dot_general x1, matrix products: 24.2 us -> 21.6 us  [column_step(): jnp.einsum('rs,nsf->nrf', reaction_rates, amounts_on_chip, precision=lax....]
  transfers between devices with their start and end apart: 7 -> 7, of which waited for: 1 -> 0; matrix products, arithmetic and copies ran while one was open for 51% -> 33% of each run, Pallas kernels for 0% -> 0%
where the time goes in v1:
time: 185 us; the launch traced here: 184 us
  local copies, waits for them, and re-layouts  49 us (26%)
  other arithmetic  40.5 us (22%)
  blocking collectives  37.5 us (20%)
  starting transfers between devices  27.2 us (15%)
  matrix products  25.2 us (14%)
  between operations  4.44 us (2%)
    unnamed x4, blocking collectives  37.5 us
    dot_general x1, matrix products, column_step(): jnp.einsum('rs,nsf->nrf', reaction_rates, amounts_on_chip, precision=lax....  21.6 us
    slice x4, local copies, waits for them, and re-layouts, level_below(): return jnp.concatenate([values[..., 64:], values[..., -64:]], axis=-1)  13.4 us
    unnamed x60, local copies, waits for them, and re-layouts  10.4 us
    reshape x1, other arithmetic, on_device(): solute_final = jnp.where(valid[:, None] > 0, new + shift[None, :, None],...  9.28 us
    all_to_all x1, starting transfers between devices, on_device(): lax.all_to_all(packed_count.reshape(device_groups, slot_limit), GY, split...  8.86 us
    all_to_all x1, starting transfers between devices, on_device(): lax.all_to_all(packed.reshape(device_groups, slot_limit, packed.shape[1])...  7.27 us
    mul x1, other arithmetic, column_step(): (kappa_flat.astype(jnp.float32) * active)[:, None]  7.26 us
  transfers between devices with their start and end apart: 7, of which 0 were waited for; matrix products, arithmetic and copies ran while one was open for 33% of the time, Pallas kernels for 0%

profile of v1, /device:TPU:0, one launch (start us, length us, event | category | flops | bytes accessed | tf_op | source)
XLA Modules:
  0.0 183.9 jit_solution(6688187778934899916)
XLA Ops:
  1.6 1.5 fusion.17
  3.5 3.5 %collective-permute-start = (f32[33,32,1]{0,1,2:T(8,128)S(1)}, f32[33,32,1]{0,1,2:T(8,128)S(1)}, u32[]{:S(2)}, u32[]{:S(2)}) collective-permute-start(f32[33,32,1]{0,1,2:T(8,128)S(1)} %copy.106), channel_id=1, source_target_pairs={{0,1},{1,2},{2,3},{3,4},{4,5},{5,6},{6,7},{7,8},{8,9},{9,10},{10,1... | collective-permute-start | bytes 12680 | tf_op jit(solution)/shard_map/ppermute | solution.py:26
  9.7 1.5 collective-permute-start.1
  15.5 8.9 %all-to-all-start = ((s32[16,1,8]{2,1,0:T(1,128)}), s32[16,1,8]{2,1,0:T(1,128)S(1)}, u32[]{:S(2)}, u32[]{:S(2)}) async-start(s32[16,1,8]{2,1,0:T(1,128)} %bitcast.8), calls=%async_computation | async-start | bytes 16384 | tf_op jit(solution)/shard_map/all_to_all | solution.py:193
  24.4 4.8 %fusion.9 = f32[128,1,2048]{2,1,0:T(1,128)S(1)} fusion(f32[128,8,2048]{2,1,0:T(8,128)} %bitcast.89), kind=kLoop, calls=%fused_computation.21 | loop fusion | flops 524288 | bytes 2097152 | tf_op jit(solution)/shard_map/add | solution.py:101
  36.6 2.0 %fusion.45 = (bf16[32,32,128]{2,1,0:T(8,128)(2,1)}, f32[32,32,128]{2,1,0:T(8,128)}) fusion(f32[32,32,128]{2,1,0:T(8,128)S(1)} %copy-done.2, f32[33,34,1]{2,1,0:T(8,128)S(1)} %pad.14, f32[33,1,128]{2,1,0:T(1,128)S(1)} %collective-permute-done.2, f32[1,32,128]{2,1,0:T(8,128)S(1)} %copy.105, f32[33,1,128]{2,1,0:T(1,128)S(1)} %collective-permute-done.1, ...), kind=kLoop, calls=%fused_computation.108 | loop fusion | flops 3538944 | bytes 3991312 | tf_op jit(solution)/shard_map/convert_element_type | solution.py:155
  38.6 2.3 %copy.111 = bf16[32,32,128]{0,2,1:T(8,128)(2,1)} copy(bf16[32,32,128]{2,1,0:T(8,128)(2,1)} %get-tuple-element.20) | data formatting | bytes 524288 | tf_op jit(solution)/shard_map/convert_element_type | solution.py:155
  40.9 4.9 %copy.112 = bf16[4,16,32,8,8]{1,0,4,3,2:T(4,128)(2,1)S(1)} copy(bf16[4,16,32,8,8]{2,4,1,3,0:T(8,128)(2,1)} %bitcast.97) | data formatting | bytes 524288 | tf_op jit(solution)/shard_map/transpose | solution.py:158
  45.9 1.7 reshape.255
  50.9 2.5 %convolution_convert_fusion = bf16[128,4160]{0,1:T(8,128)(2,1)} fusion(bf16[64,64]{0,1:T(8,128)(2,1)S(1)} %reshape.257, bf16[64,2048]{0,1:T(8,128)(2,1)S(1)} %fusion.14, bf16[64,2048]{0,1:T(8,128)(2,1)} %reshape.255, s32[64]{0:T(128)S(1)} %multiply_add_fusion), kind=kOutput, calls=%fused_computation.8 | convolution fusion | flops 70295552 | bytes 1597696 | tf_op jit(solution)/shard_map/sb,bf->sf/dot_general | solution.py:181
  53.5 2.4 %copy.115 = bf16[128,4160]{1,0:T(8,128)(2,1)} copy(bf16[128,4160]{0,1:T(8,128)(2,1)} %convolution_convert_fusion) | data formatting | bytes 2129920 | tf_op jit(solution)/shard_map/convert_element_type | solution.py:181
  55.8 7.3 %all-to-all-start.1 = ((bf16[16,8,4160]{2,1,0:T(8,128)(2,1)}), bf16[16,8,4160]{2,1,0:T(8,128)(2,1)}, u32[]{:S(2)}, u32[]{:S(2)}) async-start(bf16[16,8,4160]{2,1,0:T(8,128)(2,1)} %bitcast.96), calls=%async_computation.1 | async-start | bytes 2162688 | tf_op jit(solution)/shard_map/all_to_all | solution.py:186
  63.3 9.4 %slice.148 = f32[128,8,1984]{2,1,0:T(8,128)} slice(f32[128,8,2048]{2,1,0:T(8,128)} %bitcast.90), slice={[0:128], [0:8], [64:2048]} | slice | bytes 16252928 | tf_op jit(solution)/shard_map/slice | solution.py:58
  72.7 2.0 %slice.149 = f32[128,8,64]{2,1,0:T(8,128)} slice(f32[128,8,2048]{2,1,0:T(8,128)} %bitcast.91), slice={[0:128], [0:8], [1984:2048]} | slice | bytes 524288 | tf_op jit(solution)/shard_map/slice | solution.py:58
  84.6 4.6 %add_divide_fusion = (f32[128,2048]{1,0:T(8,128)S(1)}, bf16[16,8,2048]{2,1,0:T(8,128)(2,1)}, f32[128,2048]{1,0:T(8,128)S(1)}, f32[]{:T(128)}, f32[128,2048]{1,0:T(8,128)S(1)}) fusion(f32[128,2048]{1,0:T(8,128)} %copy.117, f32[128,2048]{1,0:T(8,128)} %copy-done.5, f32[128,1024]{1,0:T(8,128)} %slice.146, bf16[128,4160]{1,0:T(8,128)(2,1)} %bitcast.15, ...), kind=kLoop, calls=%fused_computation.29 | loop fusion | flops 5505023 | bytes 8405508 | tf_op jit(solution)/shard_map/div | solution.py:106
  89.3 7.3 %fusion = f32[128,8,2048]{2,1,0:T(8,128)} fusion(f32[128,8,64]{2,1,0:T(8,128)} %slice.149, f32[128,8,1984]{2,1,0:T(8,128)S(1)} %copy-done.1, f32[128,2048]{1,0:T(8,128)S(1)} %get-tuple-element.24, f32[1,1,128,8,2048]{4,3,2,1,0:T(8,128)} %param.14), kind=kLoop, calls=%fused_computation.1 | loop fusion | flops 6291456 | bytes 26214400 | tf_op jit(solution)/shard_map/mul | solution.py:110
  96.6 21.6 %multiply_reduce_fusion = (f32[8]{0:T(128)S(1)}, f32[8]{0:T(128)S(1)}, f32[128,8,2048]{2,1,0:T(8,128)}) fusion(f32[128,2048]{1,0:T(8,128)S(1)} %get-tuple-element.32, f32[1,1,128,8,2048]{4,3,2,1,0:T(8,128)S(1)} %bitcast.93, f32[8,8]{1,0:T(8,128)S(1)} %copy-done, f32[128,2048]{1,0:T(8,128)S(1)} %get-tuple-element.22, f32[128,8,2048]{2,1,0:T(8,128)} %fusion, ...), kind=kOutput, calls=%fused_computation.6 | convolution fusion | flops 220200944 | bytes 36438336 | tf_op jit(solution)/shard_map/rs,nsf->nrf/dot_general | solution.py:107
  118.7 1.4 dynamic-update-slice.8
  120.1 13.7 %all-reduce.22 = (f32[32]{0:T(128)S(1)}, f32[32]{0:T(128)S(1)}, f32[4]{0:T(128)S(1)}) all-reduce(f32[32]{0:T(128)S(1)} %dynamic-update-slice, f32[32]{0:T(128)S(1)} %dynamic-update-slice.4, f32[4]{0:T(128)S(1)} %dynamic-update-slice.8), channel_id=2, replica_groups=mesh['gx_0'=4,'gx_1'=2,'gy_0'=4,'gy_1'=4] {'gx_0'}, use_global_device_ids=true, to_apply=%add.8 | all-reduce | flops 68 | bytes 544
  136.5 2.7 %all-reduce.23 = (f32[16]{0:T(128)S(1)}, f32[16]{0:T(128)S(1)}, f32[2]{0:T(128)S(1)}) all-reduce(f32[16]{0:T(128)S(1)} %dynamic-update-slice.1, f32[16]{0:T(128)S(1)} %dynamic-update-slice.5, f32[2]{0:T(128)S(1)} %dynamic-update-slice.9), channel_id=3, replica_groups=mesh['gx_0'=4,'gx_1'=2,'gy_0'=4,'gy_1'=4] {'gx_1'}, use_global_device_ids=true, to_apply=%add.9 | all-reduce | flops 34 | bytes 272
  141.8 10.8 %all-reduce.21 = (f32[32]{0:T(128)S(1)}, f32[32]{0:T(128)S(1)}, f32[4]{0:T(128)S(1)}) all-reduce(f32[32]{0:T(128)S(1)} %dynamic-update-slice.2, f32[32]{0:T(128)S(1)} %dynamic-update-slice.6, f32[4]{0:T(128)S(1)} %dynamic-update-slice.10), channel_id=4, replica_groups=mesh['gx_0'=4,'gx_1'=2,'gy_0'=4,'gy_1'=4] {'gy_0'}, use_global_device_ids=true, to_apply=%add.10 | all-reduce | flops 68 | bytes 544
  155.3 10.4 %all-reduce.20 = (f32[32]{0:T(128)S(1)}, f32[32]{0:T(128)S(1)}, f32[4]{0:T(128)S(1)}) all-reduce(f32[32]{0:T(128)S(1)} %dynamic-update-slice.3, f32[32]{0:T(128)S(1)} %dynamic-update-slice.7, f32[4]{0:T(128)S(1)} %dynamic-update-slice.11), channel_id=5, replica_groups=mesh['gx_0'=4,'gx_1'=2,'gy_0'=4,'gy_1'=4] {'gy_1'}, use_global_device_ids=true, to_apply=%add.11 | all-reduce | flops 68 | bytes 544
  165.8 3.6 %all-to-all-start.2 = ((bf16[16,8,2048]{2,1,0:T(8,128)(2,1)}), bf16[16,8,2048]{2,1,0:T(8,128)(2,1)S(1)}, u32[]{:S(2)}, u32[]{:S(2)}) async-start(bf16[16,8,2048]{2,1,0:T(8,128)(2,1)} %get-tuple-element.23), calls=%async_computation.2 | async-start | bytes 1048576 | tf_op jit(solution)/shard_map/all_to_all | solution.py:232
  170.8 9.3 %select_bitcast_fusion = f32[1,1,128,8,2048]{4,3,2,1,0:T(8,128)} fusion(f32[128,8,2048]{2,1,0:T(8,128)} %get-tuple-element.33, f32[8]{0:T(128)S(1)} %subtract_divide_fusion, pred[128,2048]{1,0:T(8,128)(4,1)S(1)} %get-tuple-element.31, f32[1,1,128,8,2048]{4,3,2,1,0:T(8,128)} %param.14), kind=kLoop, calls=%fused_computation.5 | loop fusion | flops 4194304 | bytes 25428000 | tf_op jit(solution)/shard_map/reshape | solution.py:231
  (143 shorter events, 39.4 us)
Async XLA Ops:
  0.6 96.0 %copy-start = (f32[8,8]{1,0:T(8,128)S(1)}, f32[8,8]{1,0:T(8,128)}, u32[]{:S(2)}) copy-start(f32[8,8]{1,0:T(8,128)} %param.15) | copy-start | bytes 772
  3.5 27.9 %collective-permute-start = (f32[33,32,1]{0,1,2:T(8,128)S(1)}, f32[33,32,1]{0,1,2:T(8,128)S(1)}, u32[]{:S(2)}, u32[]{:S(2)}) collective-permute-start(f32[33,32,1]{0,1,2:T(8,128)S(1)} %copy.106), channel_id=1, source_target_pairs={{0,1},{1,2},{2,3},{3,4},{4,5},{5,6},{6,7},{7,8},{8,9},{9,10},{10,1... | collective-permute-start | bytes 12680 | tf_op jit(solution)/shard_map/ppermute | solution.py:26
  7.4 26.4 %collective-permute-start.3 = (f32[33,32,1]{0,1,2:T(8,128)S(1)}, f32[33,32,1]{0,1,2:T(8,128)S(1)}, u32[]{:S(2)}, u32[]{:S(2)}) collective-permute-start(f32[33,32,1]{0,1,2:T(8,128)S(1)} %copy.108), channel_id=1, source_target_pairs={{1,0},{2,1},{3,2},{4,3},{5,4},{6,5},{7,6},{8,7},{9,8},{10,9},{11,1... | collective-permute-start | bytes 12680 | tf_op jit(solution)/shard_map/ppermute | solution.py:27
  9.7 26.6 %collective-permute-start.1 = (f32[33,1,128]{2,1,0:T(1,128)S(1)}, f32[33,1,128]{2,1,0:T(1,128)S(1)}, u32[]{:S(2)}, u32[]{:S(2)}) collective-permute-start(f32[33,1,128]{2,1,0:T(1,128)S(1)} %get-tuple-element.27), channel_id=1, source_target_pairs={{0,16},{16,32},{32,48},{48,64},{64,80},{80,96},{96,112},{1,17},{17... | collective-permute-start | bytes 50696 | tf_op jit(solution)/shard_map/ppermute | solution.py:26
  11.2 25.2 %collective-permute-start.2 = (f32[33,1,128]{2,1,0:T(1,128)S(1)}, f32[33,1,128]{2,1,0:T(1,128)S(1)}, u32[]{:S(2)}, u32[]{:S(2)}) collective-permute-start(f32[33,1,128]{2,1,0:T(1,128)S(1)} %get-tuple-element.28), channel_id=1, source_target_pairs={{16,0},{32,16},{48,32},{64,48},{80,64},{96,80},{112,96},{17,1},{33... | collective-permute-start | bytes 50696 | tf_op jit(solution)/shard_map/ppermute | solution.py:27
  15.5 40.3 %all-to-all-start = ((s32[16,1,8]{2,1,0:T(1,128)}), s32[16,1,8]{2,1,0:T(1,128)S(1)}, u32[]{:S(2)}, u32[]{:S(2)}) async-start(s32[16,1,8]{2,1,0:T(1,128)} %bitcast.8), calls=%async_computation | async-start | bytes 16384 | tf_op jit(solution)/shard_map/all_to_all | solution.py:193
  24.4 6.1 %copy-start.7 = (bf16[32,128]{1,0:T(8,128)(2,1)S(1)}, bf16[32,128]{1,0:T(8,128)(2,1)}, u32[]{:S(2)}) copy-start(bf16[32,128]{1,0:T(8,128)(2,1)} %param.9) | copy-start | bytes 24580
  29.2 1.7 copy-start.8
  30.1 6.3 %copy-start.2 = (f32[32,32,128]{2,1,0:T(8,128)S(1)}, f32[32,32,128]{2,1,0:T(8,128)}, u32[]{:S(2)}) copy-start(f32[32,32,128]{2,1,0:T(8,128)} %param.8) | copy-start | bytes 1572868
  30.5 10.5 %copy-start.3 = (f32[128,2048]{1,0:T(8,128)}, f32[128,2048]{1,0:T(8,128)S(1)}, u32[]{:S(2)}) copy-start(f32[128,2048]{1,0:T(8,128)S(1)} %pad_add_fusion.2) | copy-start | bytes 3145732
  47.7 15.5 %copy-start.4 = (f32[128,2048]{1,0:T(8,128)S(1)}, f32[128,2048]{1,0:T(8,128)}, u32[]{:S(2)}) copy-start(f32[128,2048]{1,0:T(8,128)} %copy-done.3) | copy-start | bytes 3145732
  47.7 15.5 %slice-start.2 = ((f32[128,2048]{1,0:T(8,128)}), f32[128,1536]{1,0:T(8,128)S(1)}, s32[]{:S(2)}) async-start(f32[128,2048]{1,0:T(8,128)} %copy-done.3), calls=%async_computation.5 | async-start | bytes 1572864 | tf_op jit(solution)/shard_map/slice | solution.py:70
  55.8 26.5 %all-to-all-start.1 = ((bf16[16,8,4160]{2,1,0:T(8,128)(2,1)}), bf16[16,8,4160]{2,1,0:T(8,128)(2,1)}, u32[]{:S(2)}, u32[]{:S(2)}) async-start(bf16[16,8,4160]{2,1,0:T(8,128)(2,1)} %bitcast.96), calls=%async_computation.1 | async-start | bytes 2162688 | tf_op jit(solution)/shard_map/all_to_all | solution.py:186
  63.2 11.5 %copy-start.5 = (f32[128,2048]{1,0:T(8,128)}, f32[128,2048]{1,0:T(8,128)S(1)}, u32[]{:S(2)}) copy-start(f32[128,2048]{1,0:T(8,128)S(1)} %pad_add_fusion.1) | copy-start | bytes 3145732
  63.3 12.3 %copy-start.12 = (u32[128]{0:T(128)S(1)}, u32[128]{0:T(128)}, u32[]{:S(2)}) copy-start(u32[128]{0:T(128)} %constant.76) | copy-start | bytes 1540
  63.3 13.0 %copy-start.11 = (u32[128]{0:T(128)S(1)}, u32[128]{0:T(128)}, u32[]{:S(2)}) copy-start(u32[128]{0:T(128)} %constant.81) | copy-start | bytes 1540
  63.3 14.9 %copy-start.10 = (u32[128]{0:T(128)S(1)}, u32[128]{0:T(128)}, u32[]{:S(2)}) copy-start(u32[128]{0:T(128)} %constant.86) | copy-start | bytes 1540
  63.3 16.2 %copy-start.9 = (u32[128]{0:T(128)S(1)}, u32[128]{0:T(128)}, u32[]{:S(2)}) copy-start(u32[128]{0:T(128)} %constant.91) | copy-start | bytes 1540
  84.6 4.7 %copy-start.1 = (f32[128,8,1984]{2,1,0:T(8,128)S(1)}, f32[128,8,1984]{2,1,0:T(8,128)}, u32[]{:S(2)}) copy-start(f32[128,8,1984]{2,1,0:T(8,128)} %slice.148) | copy-start | bytes 24379396
  84.6 11.9 %slice-start = ((s8[8388608]{0:T(1024)(128)(4,1)}), s8[4194304]{0:T(1024)(128)(4,1)S(1)}, s32[]{:S(2)}) async-start(s8[8388608]{0:T(1024)(128)(4,1)} %bitcast.92), calls=%async_computation.3 | async-start | bytes 8388608
  89.3 7.3 %slice-start.1 = ((s8[8388608]{0:T(1024)(128)(4,1)}), s8[4194304]{0:T(1024)(128)(4,1)S(1)}, s32[]{:S(2)}) async-start(s8[8388608]{0:T(1024)(128)(4,1)} %bitcast.92), calls=%async_computation.4 | async-start | bytes 8388608
  165.8 14.3 %all-to-all-start.2 = ((bf16[16,8,2048]{2,1,0:T(8,128)(2,1)}), bf16[16,8,2048]{2,1,0:T(8,128)(2,1)S(1)}, u32[]{:S(2)}, u32[]{:S(2)}) async-start(bf16[16,8,2048]{2,1,0:T(8,128)(2,1)} %get-tuple-element.23), calls=%async_computation.2 | async-start | bytes 1048576 | tf_op jit(solution)/shard_map/all_to_all | solution.py:232
  180.1 2.9 %copy-start.6 = (f32[32,32,128]{2,1,0:T(8,128)S(1)}, f32[32,32,128]{2,1,0:T(8,128)}, u32[]{:S(2)}) copy-start(f32[32,32,128]{2,1,0:T(8,128)} %get-tuple-element.21) | copy-start | bytes 1572868
